TPU v7x, 512 devices: a whole 4x4x16 slice. The times are simulated.
512 devices in a mesh: mem: 16 (over z_lo, core), lat: 32 (over x, y, z_hi).
Axes of the slice: x: 4, y: 4, z: 16 (z_hi: 2, z_lo: 8; z = z_hi * 8 + z_lo), core: 2. Of those that a mesh axis runs over, the one named last changes fastest.
Arguments:
- control: bfloat16 [32, 10, 704, 1440], P('mem', None, 'lat'), may hold values from -6 to 6
- perturb: bfloat16 [32, 10, 704, 1440], P('mem', None, None, 'lat'), may hold values from -6 to 6
- lon_loc: bfloat16 [1440, 1440], P(None, 'mem'), may hold values from 0 to 1, as said below
- lat_loc: bfloat16 [704, 704], P('mem'), may hold values from 0 to 1, as said below
- static_scale: float32 [10, 704, 1440], P(None, 'mem', 'lat'), may hold values from 0.3 to 1
- static_field: float32 [10, 704, 1440], P(None, 'mem', 'lat'), may hold values from -6 to 6
- courant: float32 [2, 704, 1440], P(None, 'mem', 'lat'), may hold values from -0.48 to 0.48
Outputs:
- increment: float32 [10, 704, 1440], P(None, 'mem', 'lat')
- evolved: float32 [10, 704, 1440], P(None, 'mem', 'lat')
Inputs may be any that keep to these rules, and one draw needn't show every extreme that they name: `lon_loc`: Symmetric, with positive entries. `lat_loc`: Symmetric, with positive entries.
All inputs are finite; a program needn't handle non-finite values.
Results may differ from a plain program's by a relative error of at most 0.0027.
Values may be sent and summed in bfloat16 or wider, within the bound.
A program may use at most 64 MiB of HBM per device.

v0:
```python
import math
import jax
import jax.numpy as jnp
from jax import lax
from jax.sharding import PartitionSpec as P

NLAT = 704
STEPS = 4


def padded_2(shard, sides, width, wrap):
    for axis, dim in sides:
        size, length = (lax.axis_size(axis), shard.shape[dim])
        up = [(i, (i + 1) % size) for i in range(size if wrap else size - 1)]
        down = [(j, i) for i, j in up]
        last = lax.slice_in_dim(shard, length - width, length, axis=dim)
        leading = lax.slice_in_dim(shard, 0, width, axis=dim)
        before = lax.ppermute(last, axis, up)
        after = lax.ppermute(leading, axis, down)
        shard = jnp.concatenate([before, shard, after], axis=dim)
    return shard


def in_order(parts, dim):
    shape = list(parts.shape[1:])
    shape[dim] *= parts.shape[0]
    return jnp.moveaxis(parts, 0, dim).reshape(shape)


def sent_to_all(shard, axis):
    length = lax.axis_size(axis)
    return lax.all_to_all(
        jnp.broadcast_to(shard[None], (length, *shard.shape)), axis, 0, 0, tiled=True
    )


def collect(shard, axis, dim):
    return in_order(sent_to_all(shard, axis), dim)


def upwind(padded, east_west, north_south):
    center = padded[:, 1:-1, 1:-1]
    western = padded[:, 1:-1, :-2]
    eastern = padded[:, 1:-1, 2:]
    southern = padded[:, :-2, 1:-1]
    northern = padded[:, 2:, 1:-1]
    zonal = jnp.maximum(east_west, 0.0) * (center - western) + jnp.minimum(east_west, 0.0) * (
        eastern - center
    )
    meridional = jnp.maximum(north_south, 0.0) * (center - southern) + jnp.minimum(
        north_south, 0.0
    ) * (northern - center)
    return center - zonal - meridional


def lon_rim(values, width):
    return padded_2(values, (("lat", 2),), width, True)


def lat_rim(values, width):
    return padded_2(values, (("mem", 1),), width, False)


def evolve(current, courant):
    fields = current.shape[0]
    stacked = jnp.concatenate([current, courant], axis=0)
    extended = lat_rim(lon_rim(stacked, STEPS), STEPS)
    result = extended[:fields]
    wind_ext = extended[fields:]
    for step_index in range(STEPS):
        margin = step_index + 1
        inner_wind = wind_ext[
            :, margin : wind_ext.shape[1] - margin, margin : wind_ext.shape[2] - margin
        ]
        result = upwind(result, inner_wind[0], inner_wind[1])
    return result


def per_device(control, perturb, lon_loc, lat_loc, static_scale, static_field, courant):
    along_lon = jnp.einsum(
        "mfal,lc->amfc",
        control,
        lax.all_gather(lon_loc, "mem", axis=1, tiled=True),
        preferred_element_type=jnp.float32,
    ).astype(jnp.bfloat16)
    banded = lax.all_to_all(along_lon, "lat", split_axis=3, concat_axis=0, tiled=True)
    mem_here = banded.shape[1]
    fields = banded.shape[2]
    lon_width = banded.shape[3]
    flat_band = banded.reshape(banded.shape[0], mem_here * fields * lon_width)
    pert_rows = jnp.transpose(perturb, (2, 0, 1, 3))
    lat_weights_all = collect(lat_loc, "mem", 0)
    members = mem_here * lax.axis_size("mem")
    ens_scale = 1.0 / math.sqrt(members - 1)
    rows_own = NLAT // lax.axis_size("mem")
    localized = jnp.dot(lat_weights_all, flat_band, preferred_element_type=jnp.float32)
    localized = localized.reshape(NLAT, mem_here, fields, lon_width)
    ensemble_all = jnp.transpose(
        lax.psum(jnp.sum(localized * pert_rows.astype(jnp.float32), axis=1) * ens_scale, "mem"),
        (1, 0, 2),
    )
    offset = lax.axis_index("mem") * rows_own
    ensemble = lax.dynamic_slice_in_dim(ensemble_all, offset, rows_own, 1)
    increment = ensemble + static_scale * static_field
    evolved = evolve(increment, courant)
    return (increment, evolved)


def solution(mesh):
    placed = (
        P("mem", None, "lat", None),
        P("mem", None, None, "lat"),
        P(None, "mem"),
        P("mem", None),
        P(None, "mem", "lat"),
        P(None, "mem", "lat"),
        P(None, "mem", "lat"),
    )
    return jax.shard_map(
        per_device,
        mesh=mesh,
        in_specs=placed,
        out_specs=(P(None, "mem", "lat"), P(None, "mem", "lat")),
        check_vma=False,
    )
```

profile of v0, /device:TPU:1, one launch (start us, length us, event | category | flops | bytes accessed | tf_op | source)
XLA Modules:
  0.0 541.9 jit_solution(11255603198932027136)
XLA Ops:
  7.2 0.7 all-gather.3.cloned.1.call-update
  7.9 2.0 broadcast_in_dim.2
  9.9 14.0 %all-to-all-start.1 = ((bf16[16,44,704]{2,1,0:T(8,128)(2,1)}), bf16[16,44,704]{2,1,0:T(8,128)(2,1)S(1)}, u32[]{:S(2)}, u32[]{:S(2)}) async-start(bf16[16,44,704]{2,1,0:T(8,128)(2,1)} %broadcast_in_dim.2), calls=%async_computation.1 | async-start | bytes 2359296 | tf_op jit(solution)/shard_map/all_to_all | solution.py:32
  23.9 111.8 %all-gather.3.cloned.1.call-done = bf16[16,90,1440]{2,1,0:T(8,128)(2,1)} async-done(((bf16[1,90,1440]{2,1,0:T(8,128)(2,1)}), bf16[16,90,1440]{2,1,0:T(8,128)(2,1)}) %all-gather.3.cloned.1.call-update) | async-done | bytes 4147216 | tf_op jit(solution)/shard_map/all_gather | solution.py:83
  135.8 5.9 %reshape.20 = bf16[1440,1440,1,1]{1,0,2,3:T(8,128)(2,1)} reshape(bf16[16,90,1440]{2,1,0:T(8,128)(2,1)} %all-gather.3.cloned.1.call-done) | data formatting | bytes 8294400
  141.7 6.0 %fusion.6 = bf16[22,2,10,1440]{3,0,2,1:T(8,128)(2,1)} fusion(bf16[1440,1440,1,1]{1,0,2,3:T(8,128)(2,1)} %reshape.20, bf16[2,10,22,1440]{3,0,2,1:T(2,128)(2,1)S(1)} %copy-done), kind=kOutput, calls=%fused_computation.5 | convolution fusion | flops 1825401600 | bytes 6681600 | tf_op jit(solution)/shard_map/mfal,lc->amfc/dot_general | solution.py:80
  147.7 15.6 %copy.36 = bf16[22,2,10,1440]{0,1,2,3:T(2,128)(2,1)} copy(bf16[22,2,10,1440]{3,0,2,1:T(8,128)(2,1)} %fusion.6) | data formatting | bytes 2534400 | tf_op jit(solution)/shard_map/convert_element_type | solution.py:85
  163.3 11.0 %reshape.22 = bf16[32,2,9900]{2,1,0:T(2,128)(2,1)} reshape(bf16[1440,10,2,22]{3,2,1,0:T(2,128)(2,1)} %bitcast.62) | data formatting | bytes 2534400
  174.3 1.0 copy-done.1
  175.3 12.5 %all-to-all-start = ((bf16[32,2,9900]{2,1,0:T(2,128)(2,1)}), bf16[32,2,9900]{2,1,0:T(2,128)(2,1)S(1)}, u32[]{:S(2)}, u32[]{:S(2)}) async-start(bf16[32,2,9900]{2,1,0:T(2,128)(2,1)} %reshape.22), calls=%async_computation | async-start | bytes 2555904 | tf_op jit(solution)/shard_map/all_to_all | solution.py:86
  187.9 2.3 reshape.16
  190.2 44.9 %all-to-all-done = bf16[32,2,9900]{2,1,0:T(2,128)(2,1)S(1)} async-done(((bf16[32,2,9900]{2,1,0:T(2,128)(2,1)}), bf16[32,2,9900]{2,1,0:T(2,128)(2,1)S(1)}, u32[]{:S(2)}, u32[]{:S(2)}) %all-to-all-start) | async-done | bytes 1267232 | tf_op jit(solution)/shard_map/all_to_all | solution.py:86
  235.1 7.4 %reshape.23 = bf16[1440,10,2,22]{3,2,1,0:T(2,128)(2,1)} reshape(bf16[32,2,9900]{2,1,0:T(2,128)(2,1)S(1)} %all-to-all-done) | data formatting | bytes 2534400
  242.5 25.1 %copy.53 = bf16[22,2,10,32,45]{4,2,1,0,3:T(8,128)(2,1)} copy(bf16[22,2,10,32,45]{0,1,2,4,3:T(2,128)(2,1)} %bitcast.61) | data formatting | bytes 2534400 | tf_op jit(solution)/shard_map/all_to_all | solution.py:86
  267.6 7.9 %reshape.15 = bf16[704,900]{1,0:T(8,128)(2,1)S(1)} reshape(bf16[32,22,2,10,45]{4,3,2,1,0:T(8,128)(2,1)} %bitcast.63) | data formatting | bytes 2534400 | tf_op jit(solution)/shard_map/reshape | solution.py:90
  275.5 4.3 convolution_bitcast_fusion
  279.8 3.9 reshape.17
  283.7 2.5 fusion.2
  286.2 1.2 broadcast_multiply_fusion
  287.5 0.9 copy-done.3
  288.9 206.1 %all-reduce.2.cloned.1.call-done = f32[704,10,45]{0,2,1:T(8,128)} async-done(((f32[704,10,45]{0,2,1:T(8,128)}), f32[704,10,45]{0,2,1:T(8,128)}) %all-reduce.2.cloned.1.call-update) | async-done | bytes 1267216 | tf_op jit(solution)/shard_map/psum | solution.py:99
  495.0 1.2 bitcast_add_fusion
  496.2 8.1 %collective-permute-start = (f32[12,44,4]{1,2,0:T(4,128)S(1)}, f32[12,44,4]{1,2,0:T(4,128)S(1)}, u32[]{:S(2)}, u32[]{:S(2)}) collective-permute-start(f32[12,44,4]{1,2,0:T(4,128)S(1)} %get-tuple-element.26), channel_id=1, source_target_pairs={{0,1},{1,2},{2,3},{3,4},{4,5},{5,6},{6,7},{7,8},{8,9},{9,10},{10,1... | collective-permute-start | bytes 25352 | tf_op jit(solution)/shard_map/ppermute | solution.py:18
  504.4 10.1 %collective-permute-start.1 = (f32[12,44,4]{1,2,0:T(4,128)S(1)}, f32[12,44,4]{1,2,0:T(4,128)S(1)}, u32[]{:S(2)}, u32[]{:S(2)}) collective-permute-start(f32[12,44,4]{1,2,0:T(4,128)S(1)} %get-tuple-element.27), channel_id=1, source_target_pairs={{1,0},{2,1},{3,2},{4,3},{5,4},{6,5},{7,6},{8,7},{9,8},{10,9},{11,1... | collective-permute-start | bytes 25352 | tf_op jit(solution)/shard_map/ppermute | solution.py:19
  514.5 3.4 collective-permute-done.1
  518.2 4.9 collective-permute-start.2
  523.1 7.6 %collective-permute-start.3 = (f32[12,4,53]{1,2,0:T(8,128)S(1)}, f32[12,4,53]{1,2,0:T(8,128)S(1)}, u32[]{:S(2)}, u32[]{:S(2)}) collective-permute-start(f32[12,4,53]{1,2,0:T(8,128)S(1)} %get-tuple-element.25), channel_id=1, source_target_pairs={{32,0},{64,32},{96,64},{128,96},{160,128},{192,160},{224,192},{256... | collective-permute-start | bytes 30536 | tf_op jit(solution)/shard_map/ppermute | solution.py:19
  531.2 0.9 copy.49
  532.7 0.4 fusion.20
  533.1 0.4 fusion.12
  533.5 0.3 fusion.36
  534.2 0.9 copy.50
  (37 shorter events, 2.2 us)
Async XLA Ops:
  7.2 134.5 %copy-start = (bf16[2,10,22,1440]{3,0,2,1:T(2,128)(2,1)S(1)}, bf16[2,10,22,1440]{3,0,2,1:T(2,128)(2,1)}, u32[]{:S(2)}) copy-start(bf16[2,10,22,1440]{3,0,2,1:T(2,128)(2,1)} %param.7) | copy-start | bytes 3801604
  7.2 128.6 %all-gather.3.cloned.1.call-start = ((), (), s32[]{:S(2)}) async-start(), calls=%async_computation.3 | async-start | bytes 5013504 | tf_op jit(solution)/shard_map/all_gather | solution.py:83
  9.9 164.4 %all-to-all-start.1 = ((bf16[16,44,704]{2,1,0:T(8,128)(2,1)}), bf16[16,44,704]{2,1,0:T(8,128)(2,1)S(1)}, u32[]{:S(2)}, u32[]{:S(2)}) async-start(bf16[16,44,704]{2,1,0:T(8,128)(2,1)} %broadcast_in_dim.2), calls=%async_computation.1 | async-start | bytes 2359296 | tf_op jit(solution)/shard_map/all_to_all | solution.py:32
  174.3 1.0 copy-start.1
  175.3 59.7 %all-to-all-start = ((bf16[32,2,9900]{2,1,0:T(2,128)(2,1)}), bf16[32,2,9900]{2,1,0:T(2,128)(2,1)S(1)}, u32[]{:S(2)}, u32[]{:S(2)}) async-start(bf16[32,2,9900]{2,1,0:T(2,128)(2,1)} %reshape.22), calls=%async_computation | async-start | bytes 2555904 | tf_op jit(solution)/shard_map/all_to_all | solution.py:86
  187.8 307.2 %all-reduce.2.cloned.1.call-start = ((), (), s32[]{:S(2)}) async-start(), calls=%async_computation.2 | async-start | bytes 2949120 | tf_op jit(solution)/shard_map/psum | solution.py:99
  279.8 3.9 copy-start.2
  287.5 0.9 copy-start.3
  287.5 1.1 copy-start.4
  287.5 1.3 copy-start.5
  496.2 18.3 %collective-permute-start = (f32[12,44,4]{1,2,0:T(4,128)S(1)}, f32[12,44,4]{1,2,0:T(4,128)S(1)}, u32[]{:S(2)}, u32[]{:S(2)}) collective-permute-start(f32[12,44,4]{1,2,0:T(4,128)S(1)} %get-tuple-element.26), channel_id=1, source_target_pairs={{0,1},{1,2},{2,3},{3,4},{4,5},{5,6},{6,7},{7,8},{8,9},{9,10},{10,1... | collective-permute-start | bytes 25352 | tf_op jit(solution)/shard_map/ppermute | solution.py:18
  504.4 13.6 %collective-permute-start.1 = (f32[12,44,4]{1,2,0:T(4,128)S(1)}, f32[12,44,4]{1,2,0:T(4,128)S(1)}, u32[]{:S(2)}, u32[]{:S(2)}) collective-permute-start(f32[12,44,4]{1,2,0:T(4,128)S(1)} %get-tuple-element.27), channel_id=1, source_target_pairs={{1,0},{2,1},{3,2},{4,3},{5,4},{6,5},{7,6},{8,7},{9,8},{10,9},{11,1... | collective-permute-start | bytes 25352 | tf_op jit(solution)/shard_map/ppermute | solution.py:19
  518.2 13.9 %collective-permute-start.2 = (f32[12,4,53]{1,2,0:T(8,128)S(1)}, f32[12,4,53]{1,2,0:T(8,128)S(1)}, u32[]{:S(2)}, u32[]{:S(2)}) collective-permute-start(f32[12,4,53]{1,2,0:T(8,128)S(1)} %get-tuple-element.24), channel_id=1, source_target_pairs={{0,32},{32,64},{64,96},{96,128},{128,160},{160,192},{192,224},{224... | collective-permute-start | bytes 30536 | tf_op jit(solution)/shard_map/ppermute | solution.py:18
  523.1 8.9 %collective-permute-start.3 = (f32[12,4,53]{1,2,0:T(8,128)S(1)}, f32[12,4,53]{1,2,0:T(8,128)S(1)}, u32[]{:S(2)}, u32[]{:S(2)}) collective-permute-start(f32[12,4,53]{1,2,0:T(8,128)S(1)} %get-tuple-element.25), channel_id=1, source_target_pairs={{32,0},{64,32},{96,64},{128,96},{160,128},{192,160},{224,192},{256... | collective-permute-start | bytes 30536 | tf_op jit(solution)/shard_map/ppermute | solution.py:19
Sparse Core Ops, SparseCore 0:
  10.1 125.6 all-gather.2
  287.6 207.3 all-reduce.1
where the time goes:
time: 545 us; the launch traced here: 542 us
  waiting for transfers between devices  367 us (67%)
  local copies, waits for them, and re-layouts  86 us (16%)
  starting transfers between devices  57.4 us (11%)
  between operations  14.2 us (3%)
  matrix products  10.2 us (2%)
  other arithmetic  7.06 us (1%)
    psum x1, waiting for transfers between devices, per_device(): lax.psum(jnp.sum(localized * pert_rows.astype(jnp.float32), axis=1) * ens...  206 us
    all_gather x1, waiting for transfers between devices, per_device(): lax.all_gather(lon_loc, 'mem', axis=1, tiled=True)  112 us
    all_to_all x1, waiting for transfers between devices, per_device(): lax.all_to_all(along_lon, 'lat', split_axis=3, concat_axis=0, tiled=True)  44.9 us
    unnamed x20, local copies, waits for them, and re-layouts  28.6 us
    all_to_all x1, local copies, waits for them, and re-layouts, per_device(): lax.all_to_all(along_lon, 'lat', split_axis=3, concat_axis=0, tiled=True)  25.1 us
    ppermute x2, starting transfers between devices, padded_2(): after = lax.ppermute(leading, axis, down)  17.7 us
    convert_element_type x1, local copies, waits for them, and re-layouts, per_device(): along_lon = jnp.einsum('mfal,lc->amfc', control, lax.all_gather(lon_loc,...  15.6 us
    all_to_all x1, starting transfers between devices, sent_to_all(): lax.all_to_all(jnp.broadcast_to(shard[None], (length, *shard.shape)), axi...  14 us
  transfers between devices with their start and end apart: 8, of which 4 were waited for; matrix products, arithmetic and copies ran while one was open for 8% of the time, Pallas kernels for 0%

commit v1 on v0

--- a/solution.py
+++ b/solution.py
@@ -3,6 +3,7 @@
 import jax.numpy as jnp
 from jax import lax
 from jax.sharding import PartitionSpec as P
+from jax.lax import all_to_all, axis_size
 
 NLAT = 704
 STEPS = 4
@@ -83,7 +84,10 @@
         lax.all_gather(lon_loc, "mem", axis=1, tiled=True),
         preferred_element_type=jnp.float32,
     ).astype(jnp.bfloat16)
-    banded = lax.all_to_all(along_lon, "lat", split_axis=3, concat_axis=0, tiled=True)
+    banded = jnp.concatenate(
+        all_to_all(jnp.stack(jnp.split(along_lon, axis_size("lat"), axis=3), axis=0), "lat", 0, 0),
+        axis=0,
+    )
     mem_here = banded.shape[1]
     fields = banded.shape[2]
     lon_width = banded.shape[3]

time: 545 us -> 512 us (0.939)
  local copies, waits for them, and re-layouts: 86 us -> 55.2 us
    all_to_all x1, local copies, waits for them, and re-layouts: 25.1 us -> 5.98 us  [per_device(): all_to_all(jnp.stack(jnp.split(along_lon, axis_size('lat'), axis=3), axis...]
    convert_element_type x1 -> x0, local copies, waits for them, and re-layouts: 15.6 us -> none  [per_device(): along_lon = jnp.einsum('mfal,lc->amfc', control, lax.all_gather(lon_loc,...]
    another operation x0 -> x3, local copies, waits for them, and re-layouts: none -> 12.5 us  [the longest x1 7.87 us: per_device(): flat_band = banded.reshape(banded.shape[0], mem_here * fields * lon_width)]
    psum x1, waiting for transfers between devices: 206 us -> 215 us  [per_device(): lax.psum(jnp.sum(localized * pert_rows.astype(jnp.float32), axis=1) * ens...]
    reshape x1 -> x0, local copies, waits for them, and re-layouts: 7.87 us -> none  [per_device(): flat_band = banded.reshape(banded.shape[0], mem_here * fields * lon_width)]
    all_to_all x1, waiting for transfers between devices: 44.9 us -> 37.5 us  [per_device(): all_to_all(jnp.stack(jnp.split(along_lon, axis_size('lat'), axis=3), axis...]
    unnamed x20 -> x51, local copies, waits for them, and re-layouts: 28.6 us -> 27.9 us
  transfers between devices with their start and end apart: 8 -> 8, of which waited for: 4 -> 4; matrix products, arithmetic and copies ran while one was open for 8% -> 7% of each run, Pallas kernels for 0% -> 0%
where the time goes in v1:
time: 512 us
  waiting for transfers between devices  368 us (72%)
  starting transfers between devices  57.5 us (11%)
  local copies, waits for them, and re-layouts  55.2 us (11%)
  between operations  14.5 us (3%)
  matrix products  9.08 us (2%)
  other arithmetic  7.2 us (1%)
    psum x1, waiting for transfers between devices, per_device(): lax.psum(jnp.sum(localized * pert_rows.astype(jnp.float32), axis=1) * ens...  215 us
    all_gather x1, waiting for transfers between devices, per_device(): lax.all_gather(lon_loc, 'mem', axis=1, tiled=True)  112 us
    all_to_all x1, waiting for transfers between devices, per_device(): all_to_all(jnp.stack(jnp.split(along_lon, axis_size('lat'), axis=3), axis...  37.5 us
    unnamed x51, local copies, waits for them, and re-layouts  27.9 us
    ppermute x2, starting transfers between devices, padded_2(): after = lax.ppermute(leading, axis, down)  17.7 us
    all_to_all x1, starting transfers between devices, sent_to_all(): lax.all_to_all(jnp.broadcast_to(shard[None], (length, *shard.shape)), axi...  14 us
    ppermute x2, starting transfers between devices, padded_2(): before = lax.ppermute(last, axis, up)  13.1 us
    all_to_all x1, starting transfers between devices, per_device(): all_to_all(jnp.stack(jnp.split(along_lon, axis_size('lat'), axis=3), axis...  12.5 us
  transfers between devices with their start and end apart: 8, of which 4 were waited for; matrix products, arithmetic and copies ran while one was open for 7% of the time, Pallas kernels for 0%

profile of v1, /device:TPU:1, one launch (start us, length us, event | category | flops | bytes accessed | tf_op | source)
XLA Modules:
  0.0 511.6 jit_solution(5111320219431952085)
XLA Ops:
  7.2 0.7 all-gather.3.cloned.1.call-update
  7.9 2.0 broadcast_in_dim.2
  9.9 14.0 %all-to-all-start.1 = ((bf16[16,44,704]{2,1,0:T(8,128)(2,1)}), bf16[16,44,704]{2,1,0:T(8,128)(2,1)S(1)}, u32[]{:S(2)}, u32[]{:S(2)}) async-start(bf16[16,44,704]{2,1,0:T(8,128)(2,1)} %broadcast_in_dim.2), calls=%async_computation.1 | async-start | bytes 2359296 | tf_op jit(solution)/shard_map/all_to_all | solution.py:33
  23.9 111.8 %all-gather.3.cloned.1.call-done = bf16[16,90,1440]{2,1,0:T(8,128)(2,1)} async-done(((bf16[1,90,1440]{2,1,0:T(8,128)(2,1)}), bf16[16,90,1440]{2,1,0:T(8,128)(2,1)}) %all-gather.3.cloned.1.call-update) | async-done | bytes 4147216 | tf_op jit(solution)/shard_map/all_gather | solution.py:84
  135.7 5.9 %reshape.15 = bf16[1440,1440,1,1]{1,0,2,3:T(8,128)(2,1)} reshape(bf16[16,90,1440]{2,1,0:T(8,128)(2,1)} %all-gather.3.cloned.1.call-done) | data formatting | bytes 8294400
  141.7 4.8 fusion.6
  150.5 4.5 copy.44
  155.0 9.7 %reshape.17 = bf16[32,2,9900]{2,1,0:T(2,128)(2,1)} reshape(bf16[32,22,10,2,45]{4,3,2,1,0:T(2,128)(2,1)} %bitcast.188) | data formatting | bytes 2534400
  164.7 1.0 copy-done.1
  165.7 12.5 %all-to-all-start = ((bf16[32,2,9900]{2,1,0:T(2,128)(2,1)}), bf16[32,2,9900]{2,1,0:T(2,128)(2,1)S(1)}, u32[]{:S(2)}, u32[]{:S(2)}) async-start(bf16[32,2,9900]{2,1,0:T(2,128)(2,1)} %reshape.17), calls=%async_computation | async-start | bytes 2555904 | tf_op jit(solution)/shard_map/all_to_all | solution.py:88
  178.4 2.3 reshape.11
  180.8 37.5 %all-to-all-done = bf16[32,2,9900]{2,1,0:T(2,128)(2,1)S(1)} async-done(((bf16[32,2,9900]{2,1,0:T(2,128)(2,1)}), bf16[32,2,9900]{2,1,0:T(2,128)(2,1)S(1)}, u32[]{:S(2)}, u32[]{:S(2)}) %all-to-all-start) | async-done | bytes 1267232 | tf_op jit(solution)/shard_map/all_to_all | solution.py:88
  218.2 5.4 %reshape.18 = bf16[32,22,10,2,45]{4,3,2,1,0:T(2,128)(2,1)} reshape(bf16[32,2,9900]{2,1,0:T(2,128)(2,1)S(1)} %all-to-all-done) | data formatting | bytes 2534400
  223.6 6.0 %copy.20 = bf16[32,22,2,10,45]{4,3,2,1,0:T(8,128)(2,1)} copy(bf16[32,22,2,10,45]{4,2,3,1,0:T(2,128)(2,1)} %bitcast.189) | data formatting | bytes 2534400 | tf_op jit(solution)/shard_map/all_to_all | solution.py:88
  229.6 7.9 %reshape_reshape.3 = bf16[704,900]{1,0:T(8,128)(2,1)S(1)} reshape(bf16[32,22,2,10,45]{4,3,2,1,0:T(8,128)(2,1)} %copy.20) | data formatting | bytes 2534400 | tf_op jit(solution)/shard_map/reshape;reshape | solution.py:94
  237.4 4.3 convolution_bitcast_fusion
  241.7 3.9 reshape.12
  245.7 2.7 fusion.2
  248.4 1.2 broadcast_multiply_fusion
  250.1 214.7 %all-reduce.2.cloned.1.call-done = f32[704,10,45]{0,2,1:T(8,128)} async-done(((f32[704,10,45]{0,2,1:T(8,128)}), f32[704,10,45]{0,2,1:T(8,128)}) %all-reduce.2.cloned.1.call-update) | async-done | bytes 1267216 | tf_op jit(solution)/shard_map/psum | solution.py:103
  464.8 1.2 bitcast_add_fusion
  466.0 8.1 %collective-permute-start = (f32[12,44,4]{1,2,0:T(4,128)S(1)}, f32[12,44,4]{1,2,0:T(4,128)S(1)}, u32[]{:S(2)}, u32[]{:S(2)}) collective-permute-start(f32[12,44,4]{1,2,0:T(4,128)S(1)} %get-tuple-element.24), channel_id=1, source_target_pairs={{0,1},{1,2},{2,3},{3,4},{4,5},{5,6},{6,7},{7,8},{8,9},{9,10},{10,1... | collective-permute-start | bytes 25352 | tf_op jit(solution)/shard_map/ppermute | solution.py:19
  474.1 10.1 %collective-permute-start.1 = (f32[12,44,4]{1,2,0:T(4,128)S(1)}, f32[12,44,4]{1,2,0:T(4,128)S(1)}, u32[]{:S(2)}, u32[]{:S(2)}) collective-permute-start(f32[12,44,4]{1,2,0:T(4,128)S(1)} %get-tuple-element.25), channel_id=1, source_target_pairs={{1,0},{2,1},{3,2},{4,3},{5,4},{6,5},{7,6},{8,7},{9,8},{10,9},{11,1... | collective-permute-start | bytes 25352 | tf_op jit(solution)/shard_map/ppermute | solution.py:20
  484.3 3.4 collective-permute-done.1
  487.9 4.9 collective-permute-start.2
  492.9 7.6 %collective-permute-start.3 = (f32[12,4,53]{1,2,0:T(8,128)S(1)}, f32[12,4,53]{1,2,0:T(8,128)S(1)}, u32[]{:S(2)}, u32[]{:S(2)}) collective-permute-start(f32[12,4,53]{1,2,0:T(8,128)S(1)} %get-tuple-element.23), channel_id=1, source_target_pairs={{32,0},{64,32},{96,64},{128,96},{160,128},{192,160},{224,192},{256... | collective-permute-start | bytes 30536 | tf_op jit(solution)/shard_map/ppermute | solution.py:20
  500.9 0.9 copy.31
  502.5 0.4 fusion.20
  502.9 0.4 fusion.12
  503.2 0.3 fusion.36
  503.6 0.3 fusion.28
  503.9 0.9 copy.32
  (69 shorter events, 5.9 us)
Async XLA Ops:
  7.2 134.5 %copy-start = (bf16[2,10,22,1440]{3,0,2,1:T(2,128)(2,1)S(1)}, bf16[2,10,22,1440]{3,0,2,1:T(2,128)(2,1)}, u32[]{:S(2)}) copy-start(bf16[2,10,22,1440]{3,0,2,1:T(2,128)(2,1)} %param.7) | copy-start | bytes 3801604
  7.2 128.6 %all-gather.3.cloned.1.call-start = ((), (), s32[]{:S(2)}) async-start(), calls=%async_computation.3 | async-start | bytes 5013504 | tf_op jit(solution)/shard_map/all_gather | solution.py:84
  9.9 154.8 %all-to-all-start.1 = ((bf16[16,44,704]{2,1,0:T(8,128)(2,1)}), bf16[16,44,704]{2,1,0:T(8,128)(2,1)S(1)}, u32[]{:S(2)}, u32[]{:S(2)}) async-start(bf16[16,44,704]{2,1,0:T(8,128)(2,1)} %broadcast_in_dim.2), calls=%async_computation.1 | async-start | bytes 2359296 | tf_op jit(solution)/shard_map/all_to_all | solution.py:33
  164.7 1.0 copy-start.1
  165.7 52.5 %all-to-all-start = ((bf16[32,2,9900]{2,1,0:T(2,128)(2,1)}), bf16[32,2,9900]{2,1,0:T(2,128)(2,1)S(1)}, u32[]{:S(2)}, u32[]{:S(2)}) async-start(bf16[32,2,9900]{2,1,0:T(2,128)(2,1)} %reshape.17), calls=%async_computation | async-start | bytes 2555904 | tf_op jit(solution)/shard_map/all_to_all | solution.py:88
  178.2 286.6 %all-reduce.2.cloned.1.call-start = ((), (), s32[]{:S(2)}) async-start(), calls=%async_computation.2 | async-start | bytes 2949120 | tf_op jit(solution)/shard_map/psum | solution.py:103
  241.7 3.9 copy-start.2
  245.7 4.0 copy-start.3
  245.7 4.2 copy-start.4
  248.3 1.7 copy-start.5
  466.0 18.3 %collective-permute-start = (f32[12,44,4]{1,2,0:T(4,128)S(1)}, f32[12,44,4]{1,2,0:T(4,128)S(1)}, u32[]{:S(2)}, u32[]{:S(2)}) collective-permute-start(f32[12,44,4]{1,2,0:T(4,128)S(1)} %get-tuple-element.24), channel_id=1, source_target_pairs={{0,1},{1,2},{2,3},{3,4},{4,5},{5,6},{6,7},{7,8},{8,9},{9,10},{10,1... | collective-permute-start | bytes 25352 | tf_op jit(solution)/shard_map/ppermute | solution.py:19
  474.1 13.6 %collective-permute-start.1 = (f32[12,44,4]{1,2,0:T(4,128)S(1)}, f32[12,44,4]{1,2,0:T(4,128)S(1)}, u32[]{:S(2)}, u32[]{:S(2)}) collective-permute-start(f32[12,44,4]{1,2,0:T(4,128)S(1)} %get-tuple-element.25), channel_id=1, source_target_pairs={{1,0},{2,1},{3,2},{4,3},{5,4},{6,5},{7,6},{8,7},{9,8},{10,9},{11,1... | collective-permute-start | bytes 25352 | tf_op jit(solution)/shard_map/ppermute | solution.py:20
  487.9 13.9 %collective-permute-start.2 = (f32[12,4,53]{1,2,0:T(8,128)S(1)}, f32[12,4,53]{1,2,0:T(8,128)S(1)}, u32[]{:S(2)}, u32[]{:S(2)}) collective-permute-start(f32[12,4,53]{1,2,0:T(8,128)S(1)} %get-tuple-element.22), channel_id=1, source_target_pairs={{0,32},{32,64},{64,96},{96,128},{128,160},{160,192},{192,224},{224... | collective-permute-start | bytes 30536 | tf_op jit(solution)/shard_map/ppermute | solution.py:19
  492.9 8.9 %collective-permute-start.3 = (f32[12,4,53]{1,2,0:T(8,128)S(1)}, f32[12,4,53]{1,2,0:T(8,128)S(1)}, u32[]{:S(2)}, u32[]{:S(2)}) collective-permute-start(f32[12,4,53]{1,2,0:T(8,128)S(1)} %get-tuple-element.23), channel_id=1, source_target_pairs={{32,0},{64,32},{96,64},{128,96},{160,128},{192,160},{224,192},{256... | collective-permute-start | bytes 30536 | tf_op jit(solution)/shard_map/ppermute | solution.py:20
Sparse Core Ops, SparseCore 0:
  10.1 125.6 all-gather.2
  249.8 214.9 all-reduce.1
